TPU v7x, 256 devices: a whole 4x4x8 slice. The times are simulated.
256 devices in a mesh: rep: 32 (over y, z), tp: 8 (over x, core).
Axes of the slice: x: 4, y: 4, z: 8, core: 2. Of those that a mesh axis runs over, the one named last changes fastest.
Arguments:
- reference_rows: bfloat16 [32768, 8192], P('rep', 'tp'), may hold values from -7 to 7
- critic_rows: bfloat16 [32768, 4096], P('rep', 'tp'), may hold values from -7 to 7
- segment_ids: int32 [32768], P('rep'), may hold values from -1 to 32767, as said below
- pack_dest: int32 [32, 32], P('rep'), may hold values from 0 to 31, as said below
- ref_query: bfloat16 [8192, 4096], P('rep', 'tp'), may hold values from -2 to 2
- ref_key: bfloat16 [8192, 1024], P('rep', 'tp'), may hold values from -2 to 2
- ref_value: bfloat16 [8192, 1024], P('rep', 'tp'), may hold values from -0.0625 to 0.0625
- critic_query: bfloat16 [4096, 4096], P(None, 'tp'), may hold values from -2 to 2
- critic_key: bfloat16 [4096, 1024], P(None, 'tp'), may hold values from -2 to 2
- critic_value: bfloat16 [4096, 1024], P(None, 'tp'), may hold values from -0.09375 to 0.09375
- ref_readout: bfloat16 [4096], P('tp'), may hold values from -0.09375 to 0.09375
- critic_readout: bfloat16 [4096], P('tp'), may hold values from -0.09375 to 0.09375
Outputs:
- ref_score: float32 [32768], P('rep')
- value: float32 [32768], P('rep')
Inputs may be any that keep to these rules, and one draw needn't show every extreme that they name: Each row is a permutation: block b of replica s goes to pack pack_dest[s, b]. `segment_ids`: in every aligned block of 32 slots the used rows come first and the rest hold -1; a block holds 1 to 31 used rows, and every pack receives exactly 31 used rows from some replica and exactly 512 used rows in all. A rollout is a run of consecutive used rows with one id inside one block; different rollouts have different ids.
All inputs are finite; a program needn't handle non-finite values.
Results may differ from a plain program's by a relative error of at most 0.0084.
Values may be sent and summed in bfloat16 or wider, within the bound.
No kernel may reach another device: no remote copies, remote signals or barrier semaphores. Data moves between devices by JAX's collectives and lax.ppermute only.
A program may use at most 128 MiB of HBM per device.

v0:
```python
import jax
import jax.numpy as jnp
from jax import lax
from jax.sharding import PartitionSpec as P

HD = 128


def normalize(source):
    widened = source.astype(jnp.float32)
    scale_row = lax.rsqrt(jnp.mean(widened * widened, axis=-1, keepdims=True) + 1e-05)
    return (widened * scale_row).astype(jnp.bfloat16)


def attend(queries, keys_in, values_in, segments):
    row_count = queries.shape[0]
    groups = keys_in.shape[1] // HD
    shared = queries.shape[1] // keys_in.shape[1]
    query_four = queries.reshape(row_count, groups, shared, HD)
    key_three = keys_in.reshape(row_count, groups, HD)
    value_three = values_in.reshape(row_count, groups, HD)
    scores = jnp.einsum(
        "pgjd,qgd->gjpq", query_four, key_three, preferred_element_type=jnp.float32
    ) * HD ** (-0.5)
    position = jnp.arange(row_count)
    allowed = (position[None, :] <= position[:, None]) & (segments[:, None] == segments[None, :])
    masked = jnp.where(allowed, scores, -1e30)
    row_max = jnp.max(masked, axis=-1, keepdims=True)
    powers = jnp.where(allowed, jnp.exp(masked - row_max), 0.0)
    weights = (powers / jnp.sum(powers, axis=-1, keepdims=True)).astype(jnp.bfloat16)
    mixture = jnp.einsum("gjpq,qgd->pgjd", weights, value_three, preferred_element_type=jnp.float32)
    return mixture.reshape(row_count, groups * shared * HD).astype(jnp.bfloat16)


def compact_index(segments):
    row_count = segments.shape[0]
    sort_keys = jnp.where(segments >= 0, 0, row_count).astype(jnp.int32) + jnp.arange(
        row_count, dtype=jnp.int32
    )
    return jnp.argsort(sort_keys)[: row_count // 2]


def project(normed, weight):
    return jnp.dot(normed, weight, preferred_element_type=jnp.float32).astype(jnp.bfloat16)


def body(
    reference_rows,
    critic_rows,
    segment_ids,
    pack_dest,
    ref_query,
    ref_key,
    ref_value,
    critic_query,
    critic_key,
    critic_value,
    ref_readout,
    critic_readout,
):
    replicas = lax.axis_size("rep")
    slot_count = segment_ids.shape[0]
    block_rows = slot_count // replicas
    destination = pack_dest[0]
    inverse = jnp.argsort(destination)

    def by_pack(source):
        blocks = source.reshape((replicas, block_rows) + source.shape[1:])
        return jnp.take(blocks, inverse, axis=0).reshape(source.shape)

    ref_in, critic_in, ids_in = (
        lax.all_to_all(by_pack(reference_rows), "rep", split_axis=0, concat_axis=0, tiled=True),
        lax.all_to_all(by_pack(critic_rows), "rep", split_axis=0, concat_axis=0, tiled=True),
        lax.all_to_all(by_pack(segment_ids), "rep", split_axis=0, concat_axis=0, tiled=True),
    )
    chosen = compact_index(ids_in)
    pack_ids = ids_in[chosen]
    ref_full, critic_full = (
        lax.all_gather(ref_in[chosen], "tp", axis=1, tiled=True),
        lax.all_gather(critic_in[chosen], "tp", axis=1, tiled=True),
    )
    critic_normed = normalize(critic_full)
    critic_attn = attend(
        project(critic_normed, critic_query),
        project(critic_normed, critic_key),
        project(critic_normed, critic_value),
        pack_ids,
    )
    ref_normed = normalize(ref_full)
    pieces = (
        lax.all_gather(ref_query, "rep", axis=0, tiled=True),
        lax.all_gather(ref_key, "rep", axis=0, tiled=True),
        lax.all_gather(ref_value, "rep", axis=0, tiled=True),
    )
    ref_q, ref_k, ref_v = tuple(
        (
            jnp.dot(ref_normed, weight_piece, preferred_element_type=jnp.float32)
            for weight_piece in pieces
        )
    )
    ref_attn = attend(
        ref_q.astype(jnp.bfloat16), ref_k.astype(jnp.bfloat16), ref_v.astype(jnp.bfloat16), pack_ids
    )
    ref_spread = jnp.zeros((slot_count, ref_attn.shape[1]), jnp.bfloat16).at[chosen].set(ref_attn)
    critic_spread = (
        jnp.zeros((slot_count, critic_attn.shape[1]), jnp.bfloat16).at[chosen].set(critic_attn)
    )
    ref_home, critic_home = (
        lax.all_to_all(ref_spread, "rep", split_axis=0, concat_axis=0, tiled=True),
        lax.all_to_all(critic_spread, "rep", split_axis=0, concat_axis=0, tiled=True),
    )
    ref_home = jnp.take(ref_home.reshape(replicas, block_rows, -1), destination, axis=0).reshape(
        slot_count, -1
    )
    critic_home = jnp.take(
        critic_home.reshape(replicas, block_rows, -1), destination, axis=0
    ).reshape(slot_count, -1)
    partial_value = jnp.stack(
        [
            jnp.dot(ref_home, ref_readout, preferred_element_type=jnp.float32),
            jnp.dot(critic_home, critic_readout, preferred_element_type=jnp.float32),
        ]
    )
    ordered = lax.psum(partial_value, "tp")
    ordered = jnp.where(segment_ids[None, :] >= 0, ordered, 0.0)
    return (ordered[0], ordered[1])


def solution(mesh):
    return jax.shard_map(
        body,
        mesh=mesh,
        in_specs=(
            P("rep", "tp"),
            P("rep", "tp"),
            P("rep"),
            P("rep", None),
            P("rep", "tp"),
            P("rep", "tp"),
            P("rep", "tp"),
            P(None, "tp"),
            P(None, "tp"),
            P(None, "tp"),
            P("tp"),
            P("tp"),
        ),
        out_specs=(P("rep"), P("rep")),
        check_vma=False,
    )
```

profile of v0, /device:TPU:1, one launch (start us, length us, event | category | flops | bytes accessed | tf_op | source)
XLA Modules:
  0.0 513.6 jit_solution(6631517655676095522)
XLA Ops:
  7.2 0.0 copy-start
  7.2 2.4 sort.34
  9.6 0.8 reshape.165
  10.4 0.6 gather_fusion
  10.9 0.7 bitcast_select_fusion.2
  11.6 12.0 %all-to-all-start = ((s32[32,32,1]{1,2,0:T(1,128)}), s32[32,32,1]{1,2,0:T(1,128)S(1)}, u32[]{:S(2)}, u32[]{:S(2)}) async-start(s32[32,32,1]{1,2,0:T(1,128)} %bitcast.2), calls=%async_computation | async-start | bytes 32768 | tf_op jit(solution)/shard_map/all_to_all | solution.py:74
  23.7 1.8 gather_fusion.6
  25.5 1.2 broadcast_select_fusion.1
  26.7 5.6 %all-to-all-done = s32[32,32,1]{1,2,0:T(1,128)S(1)} async-done(((s32[32,32,1]{1,2,0:T(1,128)}), s32[32,32,1]{1,2,0:T(1,128)S(1)}, u32[]{:S(2)}, u32[]{:S(2)}) %all-to-all-start) | async-done | bytes 4128 | tf_op jit(solution)/shard_map/all_to_all | solution.py:74
  32.3 3.9 all-to-all-start.3
  36.2 0.0 all-gather.16.cloned.1.call-start
  36.3 0.5 broadcast.155
  36.8 0.7 reduce.7
  37.5 0.1 all_to_all.31
  37.6 4.4 sort.35
  41.9 18.7 %all-to-all-done.3 = bf16[32,32,512]{2,1,0:T(8,128)(2,1)S(1)} async-done(((bf16[32,32,512]{2,1,0:T(8,128)(2,1)}), bf16[32,32,512]{2,1,0:T(8,128)(2,1)S(1)}, u32[]{:S(2)}, u32[]{:S(2)}) %all-to-all-start.3) | async-done | bytes 1048608 | tf_op jit(solution)/shard_map/all_to_all | solution.py:73
  60.6 2.6 gather_fusion.4
  63.2 0.0 all-gather.16.cloned.1.call-update
  63.3 0.0 all-gather.14.cloned.1.call-start
  63.3 0.0 copy-done
  63.3 2.0 gather_fusion.1
  65.4 1.8 broadcast_select_fusion
  67.2 55.1 %all_to_all.45 = bf16[32,32,1024]{2,1,0:T(8,128)(2,1)} all-to-all(bf16[32,32,1024]{2,1,0:T(8,128)(2,1)S(1)} %broadcast_select_fusion), channel_id=1, replica_groups=mesh['rep'=32,'tp'=8] {'rep'}, dimensions={0} | all-to-all | bytes 4194304 | tf_op jit(solution)/shard_map/all_to_all | solution.py:72
  122.3 5.4 %gather_fusion.2 = bf16[512,1024]{1,0:T(8,128)(2,1)} fusion(bf16[1024,1024]{1,0:T(8,128)(2,1)} %bitcast.109, s32[1024]{0:T(1024)S(1)} %pad_clamp_fusion.1), kind=kCustom, calls=%fused_computation.5 | custom fusion | bytes 2099200 | tf_op jit(solution)/shard_map/gather | solution.py:79
  127.7 0.0 all-gather.14.cloned.1.call-update
  127.7 0.0 all-gather.12.cloned.1.call-start
  127.7 0.7 all-gather.12.cloned.1.call-update
  128.4 0.0 all-gather.10.cloned.1.call-start
  128.5 0.5 all-gather.10.cloned.1.call-update
  129.0 0.0 all-gather.8.cloned.1.call-start
  129.0 0.5 all-gather.8.cloned.1.call-update
  129.6 2.8 gather_fusion.3
  132.3 0.2 fusion.26
  132.6 0.0 all-gather.16.cloned.1.call-done
  132.6 0.0 copy-start.2
  132.6 3.2 fusion.2
  135.8 0.2 copy-done.2
  136.0 4.7 convolution_convert_fusion
  140.8 40.8 %all-gather.14.cloned.1.call-done = bf16[512,8192]{1,0:T(8,128)(2,1)} async-done(((bf16[512,1024]{1,0:T(8,128)(2,1)}), bf16[512,8192]{1,0:T(8,128)(2,1)}) %all-gather.14.cloned.1.call-update) | async-done | bytes 8388624 | tf_op jit(solution)/shard_map/all_gather | solution.py:79
  181.5 5.1 fusion
  186.6 95.4 %all-gather.12.cloned.1.call-done = bf16[8192,512]{1,0:T(8,128)(2,1)} async-done(((bf16[256,512]{1,0:T(8,128)(2,1)}), bf16[8192,512]{1,0:T(8,128)(2,1)}) %all-gather.12.cloned.1.call-update) | async-done | bytes 8388624 | tf_op jit(solution)/shard_map/all_gather | solution.py:91
  282.1 11.2 %convolution_convert_fusion.1 = bf16[512,512]{0,1:T(8,128)(2,1)} fusion(bf16[8192,512]{1,0:T(8,128)(2,1)} %all-gather.12.cloned.1.call-done, bf16[512,8192]{1,0:T(8,128)(2,1)} %all-gather.14.cloned.1.call-done, f32[512]{0:T(512)S(1)} %add_rsqrt_fusion.1), kind=kOutput, calls=%fused_computation.38 | convolution fusion | flops 4307812352 | bytes 17303552 | tf_op jit(solution)/shard_map/dot_general | solution.py:97
  293.3 62.8 %all-gather.10.cloned.1.call-done = bf16[8192,128]{1,0:T(8,128)(2,1)} async-done(((bf16[256,128]{1,0:T(8,128)(2,1)}), bf16[8192,128]{1,0:T(8,128)(2,1)}) %all-gather.10.cloned.1.call-update) | async-done | bytes 2097168 | tf_op jit(solution)/shard_map/all_gather | solution.py:92
  356.1 10.2 %fusion.4 = (f32[4,512]{1,0:T(4,128)S(1)}, f32[512,512,4]{1,0,2:T(8,128)}) fusion(pred[512,512]{0,1:T(8,128)(4,1)S(1)} %fusion.26, bf16[512,4,128]{0,2,1:T(8,128)(2,1)} %bitcast.122, bf16[8192,128]{1,0:T(8,128)(2,1)} %all-gather.10.cloned.1.call-done, bf16[512,8192]{1,0:T(8,128)(2,1)} %all-gather.14.cloned.1.call-done, f32[512]{0:T(512)S(1)} %add_rsqrt_fusion.1), kind=kOutput, calls=%fused_computation.24 | convolution fusion | flops 1357969408 | bytes 15476736 | tf_op jit(solution)/shard_map/pgjd,qgd->gjpq/dot_general | solution.py:22
  366.3 9.5 %fusion.6 = (f32[4,512]{1,0:T(4,128)S(1)}, f32[4,512]{1,0:T(4,128)S(1)}, f32[512,512,4]{1,0,2:T(8,128)}) fusion(f32[512,512,4]{1,0,2:T(8,128)} %get-tuple-element.14, f32[4,512]{1,0:T(4,128)S(1)} %get-tuple-element.13, pred[512,512]{0,1:T(8,128)(4,1)S(1)} %fusion.26, bf16[512,4,128]{0,2,1:T(8,128)(2,1)S(1)} %bitcast.121, bf16[4096,128]{1,0:T(8,128)(2,1)} %param.22, ...), kind=kOutput, calls=%fused_computation.26 | convolution fusion | flops 820047872 | bytes 14444544 | tf_op jit(solution)/shard_map/pgjd,qgd->gjpq/dot_general | solution.py:22
  375.7 3.2 fusion.7
  379.0 6.6 %fusion.17 = bf16[128,4,512]{2,0,1:T(8,128)(2,1)S(1)} fusion(f32[4,512]{1,0:T(4,128)S(1)} %fusion.7, f32[4,512]{1,0:T(4,128)S(1)} %get-tuple-element.8, f32[512,512,4]{1,0,2:T(8,128)} %get-tuple-element.15, pred[512,512]{0,1:T(8,128)(4,1)S(1)} %fusion.26, bf16[4096,128]{1,0:T(8,128)(2,1)} %param.23, bf16[512,4096]{1,0:T(8,128)(2,1)} %all-gather.16.cloned.1.call-done, ...), kind=kOutput, calls=%fused_computation.37 | convolution fusion | flops 818216960 | bytes 10242048 | tf_op jit(solution)/shard_map/gjpq,qgd->pgjd/dot_general | solution.py:31
  385.6 0.2 copy.32
  385.8 3.5 scatter_custom_fusion.1
  389.4 5.3 %all-to-all-start.4 = ((bf16[32,32,512]{2,1,0:T(8,128)(2,1)}), bf16[32,32,512]{2,1,0:T(8,128)(2,1)S(1)}, u32[]{:S(2)}, u32[]{:S(2)}) async-start(bf16[32,32,512]{2,1,0:T(8,128)(2,1)} %bitcast.113), calls=%async_computation.4 | async-start | bytes 2097152 | tf_op jit(solution)/shard_map/all_to_all | solution.py:110
  394.7 42.2 %all-gather.8.cloned.1.call-done = bf16[8192,128]{1,0:T(8,128)(2,1)} async-done(((bf16[256,128]{1,0:T(8,128)(2,1)}), bf16[8192,128]{1,0:T(8,128)(2,1)}) %all-gather.8.cloned.1.call-update) | async-done | bytes 2097168 | tf_op jit(solution)/shard_map/all_gather | solution.py:93
  436.9 9.9 %fusion.14 = bf16[128,4,512]{2,0,1:T(8,128)(2,1)} fusion(f32[4,512]{1,0:T(4,128)S(1)} %get-tuple-element.7, f32[4,512]{1,0:T(4,128)S(1)} %get-tuple-element.13, f32[512,512,4]{1,0,2:T(8,128)} %get-tuple-element.14, pred[512,512]{0,1:T(8,128)(4,1)S(1)} %fusion.26, bf16[8192,128]{1,0:T(8,128)(2,1)} %all-gather.8.cloned.1.call-done, ...), kind=kOutput, calls=%fused_computation.36 | convolution fusion | flops 1361379328 | bytes 15484928 | tf_op jit(solution)/shard_map/gjpq,qgd->pgjd/dot_general | solution.py:31
  446.8 2.1 copy.28
  448.9 4.0 scatter_custom_fusion
  452.9 0.0 all-to-all-done.4
  452.9 6.5 %all-to-all-start.2 = ((bf16[32,32,512]{2,1,0:T(8,128)(2,1)}), bf16[32,32,512]{2,1,0:T(8,128)(2,1)}, u32[]{:S(2)}, u32[]{:S(2)}) async-start(bf16[32,32,512]{2,1,0:T(8,128)(2,1)} %bitcast.114), calls=%async_computation.2 | async-start | bytes 2097152 | tf_op jit(solution)/shard_map/all_to_all | solution.py:109
  459.5 1.8 gather_fusion.7
  461.3 19.5 %all-to-all-done.2 = bf16[32,32,512]{2,1,0:T(8,128)(2,1)} async-done(((bf16[32,32,512]{2,1,0:T(8,128)(2,1)}), bf16[32,32,512]{2,1,0:T(8,128)(2,1)}, u32[]{:S(2)}, u32[]{:S(2)}) %all-to-all-start.2) | async-done | bytes 1048608 | tf_op jit(solution)/shard_map/all_to_all | solution.py:109
  480.8 2.8 gather_fusion.5
  483.6 1.5 broadcast_select_fusion.3
  485.1 0.4 fusion.52
  485.5 0.4 fusion.53
  485.9 20.3 %psum.7 = f32[2,1024]{1,0:T(2,128)S(1)} all-reduce(f32[2,1024]{1,0:T(2,128)S(1)} %pad_maximum_fusion), channel_id=1, replica_groups=mesh['rep'=32,'tp'=8] {'tp'}, use_global_device_ids=true, to_apply=%region_10.12 | all-reduce | flops 2048 | bytes 16384 | tf_op jit(solution)/shard_map/psum | solution.py:124
  506.2 0.6 fusion.47
  (28 shorter events, 0.1 us)
Async XLA Ops:
  7.2 56.2 %copy-start = (bf16[1024,1024]{1,0:T(8,128)(2,1)S(1)}, bf16[1024,1024]{1,0:T(8,128)(2,1)}, u32[]{:S(2)}) copy-start(bf16[1024,1024]{1,0:T(8,128)(2,1)} %param.14) | copy-start | bytes 6291460
  11.6 20.7 %all-to-all-start = ((s32[32,32,1]{1,2,0:T(1,128)}), s32[32,32,1]{1,2,0:T(1,128)S(1)}, u32[]{:S(2)}, u32[]{:S(2)}) async-start(s32[32,32,1]{1,2,0:T(1,128)} %bitcast.2), calls=%async_computation | async-start | bytes 32768 | tf_op jit(solution)/shard_map/all_to_all | solution.py:74
  32.3 28.3 %all-to-all-start.3 = ((bf16[32,32,512]{2,1,0:T(8,128)(2,1)}), bf16[32,32,512]{2,1,0:T(8,128)(2,1)S(1)}, u32[]{:S(2)}, u32[]{:S(2)}) async-start(bf16[32,32,512]{2,1,0:T(8,128)(2,1)} %broadcast_select_fusion.1), calls=%async_computation.3 | async-start | bytes 2097152 | tf_op jit(solution)/shard_map/all_to_all | solution.py:73
  36.2 96.4 %all-gather.16.cloned.1.call-start = ((), (), s32[]{:S(2)}) async-start(), calls=%async_computation.9 | async-start | bytes 4718592 | tf_op jit(solution)/shard_map/all_gather | solution.py:80
  63.3 118.3 %all-gather.14.cloned.1.call-start = ((), (), s32[]{:S(2)}) async-start(), calls=%async_computation.8 | async-start | bytes 9437184 | tf_op jit(solution)/shard_map/all_gather | solution.py:79
  127.7 154.4 %all-gather.12.cloned.1.call-start = ((), (), s32[]{:S(2)}) async-start(), calls=%async_computation.7 | async-start | bytes 8650752 | tf_op jit(solution)/shard_map/all_gather | solution.py:91
  128.4 227.6 %all-gather.10.cloned.1.call-start = ((), (), s32[]{:S(2)}) async-start(), calls=%async_computation.6 | async-start | bytes 2162688 | tf_op jit(solution)/shard_map/all_gather | solution.py:92
  129.0 307.9 %all-gather.8.cloned.1.call-start = ((), (), s32[]{:S(2)}) async-start(), calls=%async_computation.5 | async-start | bytes 2162688 | tf_op jit(solution)/shard_map/all_gather | solution.py:93
  132.6 3.5 copy-start.2
  389.4 63.5 %all-to-all-start.4 = ((bf16[32,32,512]{2,1,0:T(8,128)(2,1)}), bf16[32,32,512]{2,1,0:T(8,128)(2,1)S(1)}, u32[]{:S(2)}, u32[]{:S(2)}) async-start(bf16[32,32,512]{2,1,0:T(8,128)(2,1)} %bitcast.113), calls=%async_computation.4 | async-start | bytes 2097152 | tf_op jit(solution)/shard_map/all_to_all | solution.py:110
  446.8 12.6 %copy-start.4 = (bf16[512]{0:T(512)(128)(2,1)S(1)}, bf16[512]{0:T(512)(128)(2,1)}, u32[]{:S(2)}) copy-start(bf16[512]{0:T(512)(128)(2,1)} %param.24) | copy-start | bytes 3076
  446.8 12.6 %copy-start.5 = (bf16[512]{0:T(512)(128)(2,1)S(1)}, bf16[512]{0:T(512)(128)(2,1)}, u32[]{:S(2)}) copy-start(bf16[512]{0:T(512)(128)(2,1)} %param.25) | copy-start | bytes 3076
  446.8 12.6 %copy-start.6 = (s32[1,32]{1,0:T(1,128)S(1)}, s32[1,32]{1,0:T(1,128)}, u32[]{:S(2)}) copy-start(s32[1,32]{1,0:T(1,128)} %param.17) | copy-start | bytes 388
  446.8 12.7 %copy-start.3 = (s32[1024]{0:T(1024)S(1)}, s32[1024]{0:T(1024)}, u32[]{:S(2)}) copy-start(s32[1024]{0:T(1024)} %param.16) | copy-start | bytes 12292
  452.9 6.6 %copy-start.1 = (bf16[32,32,512]{2,1,0:T(8,128)(2,1)}, bf16[32,32,512]{2,1,0:T(8,128)(2,1)S(1)}, u32[]{:S(2)}) copy-start(bf16[32,32,512]{2,1,0:T(8,128)(2,1)S(1)} %all-to-all-done.4) | copy-start | bytes 3145732
  452.9 27.9 %all-to-all-start.2 = ((bf16[32,32,512]{2,1,0:T(8,128)(2,1)}), bf16[32,32,512]{2,1,0:T(8,128)(2,1)}, u32[]{:S(2)}, u32[]{:S(2)}) async-start(bf16[32,32,512]{2,1,0:T(8,128)(2,1)} %bitcast.114), calls=%async_computation.2 | async-start | bytes 2097152 | tf_op jit(solution)/shard_map/all_to_all | solution.py:109
Sparse Core Ops, SparseCore 0:
  63.4 36.1 all-gather.15
  127.8 53.6 all-gather.13
  184.1 97.8 all-gather.11
  284.5 71.5 all-gather.9
  358.5 78.3 all-gather.7
where the time goes:
time: 519 us; the launch traced here: 514 us
  waiting for transfers between devices  287 us (55%)
  blocking collectives  75.4 us (15%)
  matrix products  52.9 us (10%)
  local copies, waits for them, and re-layouts  31.9 us (6%)
  starting transfers between devices  27.9 us (5%)
  other arithmetic  24.5 us (5%)
  between operations  14.3 us (3%)
    all_gather x1, waiting for transfers between devices, body(): lax.all_gather(ref_query, 'rep', axis=0, tiled=True)  95.4 us
    all_gather x1, waiting for transfers between devices, body(): lax.all_gather(ref_key, 'rep', axis=0, tiled=True)  62.8 us
    all_to_all x1, blocking collectives, body(): lax.all_to_all(by_pack(reference_rows), 'rep', split_axis=0, concat_axis=...  55.1 us
    all_gather x1, waiting for transfers between devices, body(): lax.all_gather(ref_value, 'rep', axis=0, tiled=True)  42.2 us
    all_gather x1, waiting for transfers between devices, body(): lax.all_gather(ref_in[chosen], 'tp', axis=1, tiled=True)  40.8 us
    psum x1, blocking collectives, body(): ordered = lax.psum(partial_value, 'tp')  20.3 us
    dot_general x2, matrix products, attend(): jnp.einsum('pgjd,qgd->gjpq', query_four, key_three, preferred_element_typ...  19.7 us
    all_to_all x1, waiting for transfers between devices, body(): lax.all_to_all(ref_spread, 'rep', split_axis=0, concat_axis=0, tiled=True)  19.5 us
  transfers between devices with their start and end apart: 9, of which 7 were waited for; matrix products, arithmetic and copies ran while one was open for 19% of the time, Pallas kernels for 0%

commit v1 on v0

--- a/solution.py
+++ b/solution.py
@@ -90,7 +90,9 @@
     pieces = (
         lax.all_gather(ref_query, "rep", axis=0, tiled=True),
         lax.all_gather(ref_key, "rep", axis=0, tiled=True),
-        lax.all_gather(ref_value, "rep", axis=0, tiled=True),
+        jnp.concatenate(
+            lax.all_to_all(jnp.stack([ref_value] * lax.axis_size("rep")), "rep", 0, 0), axis=0
+        ),
     )
     ref_q, ref_k, ref_v = tuple(
         (

time: 519 us -> 481 us (0.927)
  waiting for transfers between devices: 287 us -> 238 us
  starting transfers between devices: 27.9 us -> 39 us
    all_gather x1 -> x0, waiting for transfers between devices: 42.2 us -> none  [body(): lax.all_gather(ref_value, 'rep', axis=0, tiled=True)]
    all_gather x1, waiting for transfers between devices: 40.8 us -> 30.6 us  [body(): lax.all_gather(ref_in[chosen], 'tp', axis=1, tiled=True)]
    all_to_all x0 -> x1, starting transfers between devices: none -> 8.16 us  [body(): lax.all_to_all(jnp.stack([ref_value] * lax.axis_size('rep')), 'rep', 0, 0)]
    all_to_all x1, waiting for transfers between devices: 0.01 us -> 6.38 us  [body(): lax.all_to_all(critic_spread, 'rep', split_axis=0, concat_axis=0, tiled=T...]
  transfers between devices with their start and end apart: 9 -> 9, of which waited for: 7 -> 7; matrix products, arithmetic and copies ran while one was open for 19% -> 20% of each run, Pallas kernels for 0% -> 0%
where the time goes in v1:
time: 481 us; the launch traced here: 475 us
  waiting for transfers between devices  238 us (49%)
  blocking collectives  76.3 us (16%)
  matrix products  52.1 us (11%)
  starting transfers between devices  39 us (8%)
  local copies, waits for them, and re-layouts  30.3 us (6%)
  other arithmetic  25.2 us (5%)
  between operations  14.3 us (3%)
    all_gather x1, waiting for transfers between devices, body(): lax.all_gather(ref_query, 'rep', axis=0, tiled=True)  95.4 us
    all_gather x1, waiting for transfers between devices, body(): lax.all_gather(ref_key, 'rep', axis=0, tiled=True)  62.8 us
    all_to_all x1, blocking collectives, body(): lax.all_to_all(by_pack(reference_rows), 'rep', split_axis=0, concat_axis=...  54.9 us
    all_gather x1, waiting for transfers between devices, body(): lax.all_gather(ref_in[chosen], 'tp', axis=1, tiled=True)  30.6 us
    psum x1, blocking collectives, body(): ordered = lax.psum(partial_value, 'tp')  21.4 us
    dot_general x2, matrix products, attend(): jnp.einsum('pgjd,qgd->gjpq', query_four, key_three, preferred_element_typ...  19.7 us
    all_to_all x1, waiting for transfers between devices, body(): lax.all_to_all(by_pack(critic_rows), 'rep', split_axis=0, concat_axis=0,...  18.7 us
    all_to_all x1, waiting for transfers between devices, body(): lax.all_to_all(ref_spread, 'rep', split_axis=0, concat_axis=0, tiled=True)  17.4 us
  transfers between devices with their start and end apart: 9, of which 7 were waited for; matrix products, arithmetic and copies ran while one was open for 20% of the time, Pallas kernels for 0%

profile of v1, /device:TPU:1, one launch (start us, length us, event | category | flops | bytes accessed | tf_op | source)
XLA Modules:
  0.0 475.5 jit_solution(1924967933561532296)
XLA Ops:
  7.2 0.0 copy-start
  7.2 2.4 sort.34
  9.6 0.8 reshape.170
  10.4 0.6 gather_fusion
  10.9 0.7 bitcast_select_fusion.2
  11.6 12.0 %all-to-all-start = ((s32[32,32,1]{1,2,0:T(1,128)}), s32[32,32,1]{1,2,0:T(1,128)S(1)}, u32[]{:S(2)}, u32[]{:S(2)}) async-start(s32[32,32,1]{1,2,0:T(1,128)} %bitcast.2), calls=%async_computation | async-start | bytes 32768 | tf_op jit(solution)/shard_map/all_to_all | solution.py:74
  23.7 1.8 gather_fusion.6
  25.5 1.2 broadcast_select_fusion.1
  26.7 5.6 %all-to-all-done = s32[32,32,1]{1,2,0:T(1,128)S(1)} async-done(((s32[32,32,1]{1,2,0:T(1,128)}), s32[32,32,1]{1,2,0:T(1,128)S(1)}, u32[]{:S(2)}, u32[]{:S(2)}) %all-to-all-start) | async-done | bytes 4128 | tf_op jit(solution)/shard_map/all_to_all | solution.py:74
  32.3 3.9 all-to-all-start.4
  36.2 0.0 all-gather.13.cloned.1.call-start
  36.3 0.5 broadcast.157
  36.8 0.7 reduce.7
  37.5 0.1 all_to_all.34
  37.6 4.4 sort.35
  41.9 18.7 %all-to-all-done.4 = bf16[32,32,512]{2,1,0:T(8,128)(2,1)S(1)} async-done(((bf16[32,32,512]{2,1,0:T(8,128)(2,1)}), bf16[32,32,512]{2,1,0:T(8,128)(2,1)S(1)}, u32[]{:S(2)}, u32[]{:S(2)}) %all-to-all-start.4) | async-done | bytes 1048608 | tf_op jit(solution)/shard_map/all_to_all | solution.py:73
  60.6 2.6 gather_fusion.4
  63.2 0.0 all-gather.13.cloned.1.call-update
  63.3 0.0 all-gather.11.cloned.1.call-start
  63.3 2.0 gather_fusion.1
  65.4 1.8 broadcast_select_fusion
  67.2 54.9 %all_to_all.50 = bf16[32,32,1024]{2,1,0:T(8,128)(2,1)S(1)} all-to-all(bf16[32,32,1024]{2,1,0:T(8,128)(2,1)S(1)} %broadcast_select_fusion), channel_id=1, replica_groups=mesh['rep'=32,'tp'=8] {'rep'}, dimensions={0} | all-to-all | bytes 4194304 | tf_op jit(solution)/shard_map/all_to_all | solution.py:72
  122.2 2.8 gather_fusion.2
  125.0 0.0 all-gather.11.cloned.1.call-update
  125.0 0.0 all-gather.9.cloned.1.call-start
  125.1 0.7 all-gather.9.cloned.1.call-update
  125.8 0.0 all-gather.7.cloned.1.call-start
  125.8 0.5 all-gather.7.cloned.1.call-update
  126.3 1.8 stack.8
  128.1 8.2 %all-to-all-start.2 = ((bf16[32,256,128]{2,1,0:T(8,128)(2,1)}), bf16[32,256,128]{2,1,0:T(8,128)(2,1)S(1)}, u32[]{:S(2)}, u32[]{:S(2)}) async-start(bf16[32,256,128]{2,1,0:T(8,128)(2,1)} %stack.8), calls=%async_computation.2 | async-start | bytes 4194304 | tf_op jit(solution)/shard_map/all_to_all | solution.py:94
  136.3 2.8 gather_fusion.3
  139.1 0.2 fusion.26
  139.3 0.0 all-gather.13.cloned.1.call-done
  139.3 3.9 fusion.2
  143.3 0.2 copy-done.3
  143.5 4.7 convolution_convert_fusion
  148.2 30.6 %all-gather.11.cloned.1.call-done = bf16[512,8192]{1,0:T(8,128)(2,1)} async-done(((bf16[512,1024]{1,0:T(8,128)(2,1)}), bf16[512,8192]{1,0:T(8,128)(2,1)}) %all-gather.11.cloned.1.call-update) | async-done | bytes 8388624 | tf_op jit(solution)/shard_map/all_gather | solution.py:79
  178.9 5.1 %fusion = f32[512]{0:T(512)S(1)} fusion(bf16[512,8192]{1,0:T(8,128)(2,1)} %all-gather.11.cloned.1.call-done), kind=kLoop, calls=%fused_computation.12 | loop fusion | flops 12582400 | bytes 8390656 | tf_op jit(solution)/shard_map/reduce_sum | solution.py:11
  184.0 95.4 %all-gather.9.cloned.1.call-done = bf16[8192,512]{1,0:T(8,128)(2,1)} async-done(((bf16[256,512]{1,0:T(8,128)(2,1)}), bf16[8192,512]{1,0:T(8,128)(2,1)}) %all-gather.9.cloned.1.call-update) | async-done | bytes 8388624 | tf_op jit(solution)/shard_map/all_gather | solution.py:91
  279.4 11.2 %convolution_convert_fusion.1 = bf16[512,512]{0,1:T(8,128)(2,1)} fusion(bf16[8192,512]{1,0:T(8,128)(2,1)} %all-gather.9.cloned.1.call-done, bf16[512,8192]{1,0:T(8,128)(2,1)} %all-gather.11.cloned.1.call-done, f32[512]{0:T(512)S(1)} %add_rsqrt_fusion.1), kind=kOutput, calls=%fused_computation.38 | convolution fusion | flops 4307812352 | bytes 17303552 | tf_op jit(solution)/shard_map/dot_general | solution.py:99
  290.6 62.8 %all-gather.7.cloned.1.call-done = bf16[8192,128]{1,0:T(8,128)(2,1)} async-done(((bf16[256,128]{1,0:T(8,128)(2,1)}), bf16[8192,128]{1,0:T(8,128)(2,1)}) %all-gather.7.cloned.1.call-update) | async-done | bytes 2097168 | tf_op jit(solution)/shard_map/all_gather | solution.py:92
  353.4 10.2 %fusion.4 = (f32[4,512]{1,0:T(4,128)S(1)}, f32[512,512,4]{1,0,2:T(8,128)}) fusion(pred[512,512]{0,1:T(8,128)(4,1)S(1)} %fusion.26, bf16[512,4,128]{0,2,1:T(8,128)(2,1)} %bitcast.122, bf16[8192,128]{1,0:T(8,128)(2,1)} %all-gather.7.cloned.1.call-done, bf16[512,8192]{1,0:T(8,128)(2,1)} %all-gather.11.cloned.1.call-done, f32[512]{0:T(512)S(1)} %add_rsqrt_fusion.1), kind=kOutput, calls=%fused_computation.24 | convolution fusion | flops 1357969408 | bytes 15476736 | tf_op jit(solution)/shard_map/pgjd,qgd->gjpq/dot_general | solution.py:22
  363.6 9.5 %fusion.6 = (f32[4,512]{1,0:T(4,128)S(1)}, f32[4,512]{1,0:T(4,128)S(1)}, f32[512,512,4]{1,0,2:T(8,128)}) fusion(f32[512,512,4]{1,0,2:T(8,128)} %get-tuple-element.14, f32[4,512]{1,0:T(4,128)S(1)} %get-tuple-element.13, pred[512,512]{0,1:T(8,128)(4,1)S(1)} %fusion.26, bf16[512,4,128]{0,2,1:T(8,128)(2,1)S(1)} %bitcast.121, bf16[4096,128]{1,0:T(8,128)(2,1)} %param.22, ...), kind=kOutput, calls=%fused_computation.26 | convolution fusion | flops 820047872 | bytes 14444544 | tf_op jit(solution)/shard_map/pgjd,qgd->gjpq/dot_general | solution.py:22
  373.1 3.2 fusion.7
  376.3 6.6 %fusion.17 = bf16[128,4,512]{2,0,1:T(8,128)(2,1)S(1)} fusion(f32[4,512]{1,0:T(4,128)S(1)} %fusion.7, f32[4,512]{1,0:T(4,128)S(1)} %get-tuple-element.8, f32[512,512,4]{1,0,2:T(8,128)} %get-tuple-element.15, pred[512,512]{0,1:T(8,128)(4,1)S(1)} %fusion.26, bf16[4096,128]{1,0:T(8,128)(2,1)} %param.23, bf16[512,4096]{1,0:T(8,128)(2,1)} %all-gather.13.cloned.1.call-done, ...), kind=kOutput, calls=%fused_computation.37 | convolution fusion | flops 818216960 | bytes 10242048 | tf_op jit(solution)/shard_map/gjpq,qgd->pgjd/dot_general | solution.py:31
  382.9 0.2 copy.32
  383.1 3.5 scatter_custom_fusion.1
  386.6 1.4 copy-done.4
  388.0 5.3 %all-to-all-start.5 = ((bf16[32,32,512]{2,1,0:T(8,128)(2,1)}), bf16[32,32,512]{2,1,0:T(8,128)(2,1)S(1)}, u32[]{:S(2)}, u32[]{:S(2)}) async-start(bf16[32,32,512]{2,1,0:T(8,128)(2,1)} %bitcast.29), calls=%async_computation.5 | async-start | bytes 2097152 | tf_op jit(solution)/shard_map/all_to_all | solution.py:112
  393.2 9.1 %fusion.14 = bf16[128,4,512]{2,0,1:T(8,128)(2,1)S(1)} fusion(f32[4,512]{1,0:T(4,128)S(1)} %get-tuple-element.7, f32[4,512]{1,0:T(4,128)S(1)} %get-tuple-element.13, f32[512,512,4]{1,0,2:T(8,128)} %get-tuple-element.14, pred[512,512]{0,1:T(8,128)(4,1)S(1)} %fusion.26, bf16[8192,128]{1,0:T(8,128)(2,1)} %bitcast.114, ...), kind=kOutput, calls=%fused_computation.36 | convolution fusion | flops 1361379328 | bytes 15484928 | tf_op jit(solution)/shard_map/gjpq,qgd->pgjd/dot_general | solution.py:31
  402.4 0.0 copy-start.8
  402.4 0.0 copy-start.9
  402.4 0.2 copy.28
  402.7 3.5 scatter_custom_fusion
  406.1 6.4 %all-to-all-done.5 = bf16[32,32,512]{2,1,0:T(8,128)(2,1)S(1)} async-done(((bf16[32,32,512]{2,1,0:T(8,128)(2,1)}), bf16[32,32,512]{2,1,0:T(8,128)(2,1)S(1)}, u32[]{:S(2)}, u32[]{:S(2)}) %all-to-all-start.5) | async-done | bytes 1048608 | tf_op jit(solution)/shard_map/all_to_all | solution.py:112
  412.5 9.5 %all-to-all-start.3 = ((bf16[32,32,512]{2,1,0:T(8,128)(2,1)}), bf16[32,32,512]{2,1,0:T(8,128)(2,1)}, u32[]{:S(2)}, u32[]{:S(2)}) async-start(bf16[32,32,512]{2,1,0:T(8,128)(2,1)} %bitcast.15), calls=%async_computation.3 | async-start | bytes 2097152 | tf_op jit(solution)/shard_map/all_to_all | solution.py:111
  422.2 2.0 gather_fusion.7
  424.2 17.4 %all-to-all-done.3 = bf16[32,32,512]{2,1,0:T(8,128)(2,1)} async-done(((bf16[32,32,512]{2,1,0:T(8,128)(2,1)}), bf16[32,32,512]{2,1,0:T(8,128)(2,1)}, u32[]{:S(2)}, u32[]{:S(2)}) %all-to-all-start.3) | async-done | bytes 1048608 | tf_op jit(solution)/shard_map/all_to_all | solution.py:111
  441.6 2.8 gather_fusion.5
  444.4 1.5 broadcast_select_fusion.3
  445.9 0.4 fusion.52
  446.3 0.4 fusion.53
  446.7 21.4 %psum.7 = f32[2,1024]{1,0:T(2,128)S(1)} all-reduce(f32[2,1024]{1,0:T(2,128)S(1)} %pad_maximum_fusion), channel_id=1, replica_groups=mesh['rep'=32,'tp'=8] {'tp'}, use_global_device_ids=true, to_apply=%region_10.12 | all-reduce | flops 2048 | bytes 16384 | tf_op jit(solution)/shard_map/psum | solution.py:126
  468.1 0.6 fusion.47
  (34 shorter events, 0.2 us)
Async XLA Ops:
  7.2 56.2 %copy-start = (bf16[1024,1024]{1,0:T(8,128)(2,1)S(1)}, bf16[1024,1024]{1,0:T(8,128)(2,1)}, u32[]{:S(2)}) copy-start(bf16[1024,1024]{1,0:T(8,128)(2,1)} %param.14) | copy-start | bytes 6291460
  11.6 20.7 %all-to-all-start = ((s32[32,32,1]{1,2,0:T(1,128)}), s32[32,32,1]{1,2,0:T(1,128)S(1)}, u32[]{:S(2)}, u32[]{:S(2)}) async-start(s32[32,32,1]{1,2,0:T(1,128)} %bitcast.2), calls=%async_computation | async-start | bytes 32768 | tf_op jit(solution)/shard_map/all_to_all | solution.py:74
  32.3 28.3 %all-to-all-start.4 = ((bf16[32,32,512]{2,1,0:T(8,128)(2,1)}), bf16[32,32,512]{2,1,0:T(8,128)(2,1)S(1)}, u32[]{:S(2)}, u32[]{:S(2)}) async-start(bf16[32,32,512]{2,1,0:T(8,128)(2,1)} %broadcast_select_fusion.1), calls=%async_computation.4 | async-start | bytes 2097152 | tf_op jit(solution)/shard_map/all_to_all | solution.py:73
  36.2 103.1 %all-gather.13.cloned.1.call-start = ((), (), s32[]{:S(2)}) async-start(), calls=%async_computation.9 | async-start | bytes 4718592 | tf_op jit(solution)/shard_map/all_gather | solution.py:80
  63.3 115.6 %all-gather.11.cloned.1.call-start = ((), (), s32[]{:S(2)}) async-start(), calls=%async_computation.8 | async-start | bytes 9437184 | tf_op jit(solution)/shard_map/all_gather | solution.py:79
  122.2 4.2 copy-start.5
  125.0 154.4 %all-gather.9.cloned.1.call-start = ((), (), s32[]{:S(2)}) async-start(), calls=%async_computation.7 | async-start | bytes 8650752 | tf_op jit(solution)/shard_map/all_gather | solution.py:91
  125.8 227.6 %all-gather.7.cloned.1.call-start = ((), (), s32[]{:S(2)}) async-start(), calls=%async_computation.6 | async-start | bytes 2162688 | tf_op jit(solution)/shard_map/all_gather | solution.py:92
  128.1 258.5 %all-to-all-start.2 = ((bf16[32,256,128]{2,1,0:T(8,128)(2,1)}), bf16[32,256,128]{2,1,0:T(8,128)(2,1)S(1)}, u32[]{:S(2)}, u32[]{:S(2)}) async-start(bf16[32,256,128]{2,1,0:T(8,128)(2,1)} %stack.8), calls=%async_computation.2 | async-start | bytes 4194304 | tf_op jit(solution)/shard_map/all_to_all | solution.py:94
  139.3 4.2 copy-start.3
  386.6 1.4 copy-start.4
  388.0 24.5 %all-to-all-start.5 = ((bf16[32,32,512]{2,1,0:T(8,128)(2,1)}), bf16[32,32,512]{2,1,0:T(8,128)(2,1)S(1)}, u32[]{:S(2)}, u32[]{:S(2)}) async-start(bf16[32,32,512]{2,1,0:T(8,128)(2,1)} %bitcast.29), calls=%async_computation.5 | async-start | bytes 2097152 | tf_op jit(solution)/shard_map/all_to_all | solution.py:112
  402.4 19.6 %copy-start.7 = (bf16[512]{0:T(512)(128)(2,1)S(1)}, bf16[512]{0:T(512)(128)(2,1)}, u32[]{:S(2)}) copy-start(bf16[512]{0:T(512)(128)(2,1)} %param.24) | copy-start | bytes 3076
  402.4 19.6 %copy-start.8 = (bf16[512]{0:T(512)(128)(2,1)S(1)}, bf16[512]{0:T(512)(128)(2,1)}, u32[]{:S(2)}) copy-start(bf16[512]{0:T(512)(128)(2,1)} %param.25) | copy-start | bytes 3076
  402.4 19.7 %copy-start.9 = (s32[1,32]{1,0:T(1,128)S(1)}, s32[1,32]{1,0:T(1,128)}, u32[]{:S(2)}) copy-start(s32[1,32]{1,0:T(1,128)} %param.17) | copy-start | bytes 388
  402.4 19.7 %copy-start.6 = (s32[1024]{0:T(1024)S(1)}, s32[1024]{0:T(1024)}, u32[]{:S(2)}) copy-start(s32[1024]{0:T(1024)} %param.16) | copy-start | bytes 12292
  412.5 9.6 %copy-start.2 = (bf16[32,32,512]{2,1,0:T(8,128)(2,1)}, bf16[32,32,512]{2,1,0:T(8,128)(2,1)S(1)}, u32[]{:S(2)}) copy-start(bf16[32,32,512]{2,1,0:T(8,128)(2,1)S(1)} %all-to-all-done.5) | copy-start | bytes 3145732
  412.5 29.1 %all-to-all-start.3 = ((bf16[32,32,512]{2,1,0:T(8,128)(2,1)}), bf16[32,32,512]{2,1,0:T(8,128)(2,1)}, u32[]{:S(2)}, u32[]{:S(2)}) async-start(bf16[32,32,512]{2,1,0:T(8,128)(2,1)} %bitcast.15), calls=%async_computation.3 | async-start | bytes 2097152 | tf_op jit(solution)/shard_map/all_to_all | solution.py:111
  422.1 46.6 %copy-start.1 = (bf16[1024,1024]{1,0:T(8,128)(2,1)S(1)}, bf16[1024,1024]{1,0:T(8,128)(2,1)}, u32[]{:S(2)}) copy-start(bf16[1024,1024]{1,0:T(8,128)(2,1)} %param.14) | copy-start | bytes 6291460
Sparse Core Ops, SparseCore 0:
  63.4 36.1 all-gather.12
  125.1 53.6 all-gather.10
  181.5 97.8 all-gather.8
  281.8 71.5 all-gather.6
